TPU v7x, 256 devices: a whole 4x4x8 slice. The times are simulated.
256 devices in a mesh: cols: 128 (over x, y, z), rows: 2 (over core).
Axes of the slice: x: 4, y: 4, z: 8, core: 2. Of those that a mesh axis runs over, the one named last changes fastest.
Arguments:
- activations: bfloat16 [256, 65536], P('rows', 'cols'), may hold values from 0 to 16
- weights: bfloat16 [2, 512, 40, 128, 128], P(None, 'cols', 'rows'), may hold values from -0.15625 to 0.15625
- biases: float32 [2, 65536], P(None, 'cols'), may hold values from -6 to 2
- pattern: int32 [2, 512, 40], P(None, 'cols'), may hold values from 0 to 511, as said below
- counts: int32 [2, 512], P(None, 'cols'), may hold values from 1 to 40, 10240 in all within a row
Outputs:
- result: bfloat16 [256, 65536], P('rows', 'cols')
Inputs may be any that keep to these rules, and one draw needn't show every extreme that they name: `pattern`: the 40 entries of a column block are distinct. All entries of the 4 column blocks held by one index of cols, live or not, name at most 1 different blocks among the 4 blocks held by any one index of cols, and exactly 1 for some. In each layer the counts sum to 10240.
All inputs are finite; a program needn't handle non-finite values. No bound on the sum of `counts` on one device may be relied on, other than what follows from the above.
Results may differ from a plain program's by a relative error of at most 0.0047.
Values may be sent and summed in bfloat16 or wider, within the bound.
A program may use at most 128 MiB of HBM per device.

v0:
```python
import jax
import jax.numpy as jnp
from jax import lax
from jax.sharding import PartitionSpec as P


def per_device(activations, weights, biases, pattern, counts):
    rows_here = activations.shape[0]
    owned = pattern.shape[1]
    slot_count = pattern.shape[2]
    block_size = weights.shape[-1]
    layers = weights.shape[0]
    devices = lax.axis_size("cols")
    nblocks_all = owned * devices
    current = activations
    for layer in range(layers):
        weight_all = lax.all_gather(weights[layer], "rows", axis=1, tiled=True)
        live_slots = (jnp.arange(slot_count)[None, :] < counts[layer][:, None]).astype(jnp.bfloat16)
        weight_used = weight_all * live_slots[:, :, None, None]
        layer_bias = biases[layer]
        gathered = lax.all_gather(current, "cols", axis=1, tiled=True)
        all_blocks = gathered.reshape(rows_here, nblocks_all, block_size)
        selected = jnp.take(all_blocks, pattern[layer].reshape(-1), axis=1)
        items = selected.shape[0]
        picked = selected.reshape(items, owned, slot_count, block_size)
        total = jnp.einsum(
            "sjkb,jkbc->sjc", picked, weight_used, preferred_element_type=jnp.float32
        )
        shifted = total.reshape(items, owned * block_size) + layer_bias[None, :]
        current = jnp.clip(shifted, 0.0, 32.0).astype(jnp.bfloat16)
    return current


def solution(mesh):
    return jax.shard_map(
        per_device,
        mesh=mesh,
        in_specs=(
            P("rows", "cols"),
            P(None, "cols", "rows", None, None),
            P(None, "cols"),
            P(None, "cols", None),
            P(None, "cols"),
        ),
        out_specs=P("rows", "cols"),
        check_vma=False,
    )
```

profile of v0, /device:TPU:8, one launch (start us, length us, event | category | flops | bytes accessed | tf_op | source)
XLA Modules:
  0.0 414.9 jit_solution(2486084904053249132)
XLA Ops:
  6.5 0.0 all-gather.7.cloned.1.call-start
  6.5 1.7 copy.16
  8.2 0.0 all-gather.7.cloned.1.call-update
  8.2 0.0 copy-start
  8.2 0.0 copy-start.2
  8.2 0.0 copy-start.1
  8.3 0.0 all-gather.13.cloned.1.call-start
  8.3 7.0 %fusion.10 = (bf16[1,4,20,128,128]{4,3,2,1,0:T(8,128)(2,1)}, bf16[1,4,20,128,128]{4,3,2,1,0:T(8,128)(2,1)}) fusion(bf16[2,4,20,128,128]{4,3,2,1,0:T(8,128)(2,1)} %param.8), kind=kLoop, calls=%fused_computation.28 | loop fusion | bytes 10485760 | tf_op jit(solution)/shard_map/slice | solution.py:17
  15.3 0.0 all-gather.13.cloned.1.call-update
  15.3 0.0 all-gather.9.cloned.1.call-start
  15.4 0.0 copy-done
  15.4 0.1 reshape_squeeze.6
  15.5 0.1 fusion.9
  15.6 0.0 copy-done.1
  15.6 148.4 %all-gather.7.cloned.1.call-done = bf16[128,65536]{0,1:T(8,128)(2,1)} async-done(((bf16[128,512]{0,1:T(8,128)(2,1)}), bf16[128,65536]{0,1:T(8,128)(2,1)}) %all-gather.7.cloned.1.call-update) | async-done | bytes 16777232 | tf_op jit(solution)/shard_map/all_gather | solution.py:21
  164.0 22.7 %copy.17 = bf16[128,512,128]{2,0,1:T(8,128)(2,1)} copy(bf16[128,512,128]{0,2,1:T(8,128)(2,1)} %bitcast.44) | data formatting | bytes 33554432 | tf_op jit(solution)/shard_map/reshape | solution.py:22
  186.7 13.5 %gather_fusion = bf16[160,128,128]{2,1,0:T(8,128)(2,1)} fusion(bf16[128,512,128]{2,0,1:T(8,128)(2,1)} %copy.17, s32[1024]{0:T(1024)S(1)} %pad_clamp_fusion.1), kind=kCustom, calls=%fused_computation.clone | custom fusion | bytes 10486400 | tf_op jit(solution)/shard_map/jit(_take)/gather | solution.py:23
  200.1 5.3 %broadcast_select_fusion.1 = bf16[160,128,128]{2,1,0:T(8,128)(2,1)} fusion(bf16[160,128,128]{2,1,0:T(8,128)(2,1)} %gather_fusion, pred[160]{0:T(512)(128)(4,1)S(1)} %compare_and_fusion.1), kind=kLoop, calls=%fused_computation.7 | loop fusion | flops 2621440 | bytes 10485920 | tf_op jit(solution)/shard_map/jit(_take)/select_n | solution.py:23
  205.5 6.1 %fusion = f32[4,128,128,1]{2,1,3,0:T(8,128)S(1)} fusion(bf16[128,4,40,128]{3,0,2,1:T(8,128)(2,1)} %bitcast.46, bf16[1,4,40,128,128]{4,3,2,1,0:T(8,128)(2,1)} %all-gather.13.cloned.1.call-done, bf16[4,40]{1,0:T(4,128)(2,1)S(1)} %fusion.9), kind=kOutput, calls=%fused_computation.3 | convolution fusion | flops 673710080 | bytes 10748224 | tf_op jit(solution)/shard_map/sjkb,jkbc->sjc/dot_general | solution.py:26
  211.6 0.8 fusion.7
  212.4 0.0 all-gather.9.cloned.1.call-update
  212.4 0.2 all-gather.11.cloned.1.call-start
  212.7 0.3 all-gather.11.cloned.1.call-update
  213.0 0.1 reshape_squeeze.7
  213.1 0.1 fusion.8
  213.2 146.7 %all-gather.9.cloned.1.call-done = bf16[128,65536]{0,1:T(8,128)(2,1)} async-done(((bf16[128,512]{0,1:T(8,128)(2,1)}), bf16[128,65536]{0,1:T(8,128)(2,1)}) %all-gather.9.cloned.1.call-update) | async-done | bytes 16777232 | tf_op jit(solution)/shard_map/all_gather | solution.py:21
  359.9 22.7 %copy.19 = bf16[128,512,128]{2,0,1:T(8,128)(2,1)} copy(bf16[128,512,128]{0,2,1:T(8,128)(2,1)} %bitcast.45) | data formatting | bytes 33554432 | tf_op jit(solution)/shard_map/reshape | solution.py:22
  382.6 13.5 %gather_fusion.1 = bf16[160,128,128]{2,1,0:T(8,128)(2,1)} fusion(bf16[128,512,128]{2,0,1:T(8,128)(2,1)} %copy.19, s32[1024]{0:T(1024)S(1)} %pad_clamp_fusion), kind=kCustom, calls=%fused_computation.1.clone | custom fusion | bytes 10486400 | tf_op jit(solution)/shard_map/jit(_take)/gather | solution.py:23
  396.0 5.3 %broadcast_select_fusion = bf16[160,128,128]{2,1,0:T(8,128)(2,1)} fusion(bf16[160,128,128]{2,1,0:T(8,128)(2,1)} %gather_fusion.1, pred[160]{0:T(512)(128)(4,1)S(1)} %compare_and_fusion), kind=kLoop, calls=%fused_computation.6 | loop fusion | flops 2621440 | bytes 10485920 | tf_op jit(solution)/shard_map/jit(_take)/select_n | solution.py:23
  401.4 6.1 %fusion.1 = f32[4,128,128,1]{2,1,3,0:T(8,128)S(1)} fusion(bf16[128,4,40,128]{3,0,2,1:T(8,128)(2,1)} %bitcast.47, bf16[1,4,40,128,128]{4,3,2,1,0:T(8,128)(2,1)} %all-gather.11.cloned.1.call-done, bf16[4,40]{1,0:T(4,128)(2,1)S(1)} %fusion.8), kind=kOutput, calls=%fused_computation.5 | convolution fusion | flops 673710080 | bytes 10748224 | tf_op jit(solution)/shard_map/sjkb,jkbc->sjc/dot_general | solution.py:26
  407.5 0.1 fusion.5
  407.6 0.8 copy.21
  (12 shorter events, 0.1 us)
Async XLA Ops:
  6.5 157.5 %all-gather.7.cloned.1.call-start = ((), (), s32[]{:S(2)}) async-start(), calls=%async_computation | async-start | bytes 16908288 | tf_op jit(solution)/shard_map/all_gather | solution.py:21
  8.2 7.2 %copy-start = (s32[2,4,40]{2,1,0:T(4,128)S(1)}, s32[2,4,40]{2,1,0:T(4,128)}, u32[]{:S(2)}) copy-start(s32[2,4,40]{2,1,0:T(4,128)} %param.10) | copy-start | bytes 3844
  8.2 7.3 %copy-start.2 = (s32[2,4]{1,0:T(2,128)S(1)}, s32[2,4]{1,0:T(2,128)}, u32[]{:S(2)}) copy-start(s32[2,4]{1,0:T(2,128)} %param.11) | copy-start | bytes 100
  8.2 7.4 %copy-start.1 = (f32[2,512]{1,0:T(2,128)S(1)}, f32[2,512]{1,0:T(2,128)}, u32[]{:S(2)}) copy-start(f32[2,512]{1,0:T(2,128)} %param.9) | copy-start | bytes 12292
  8.3 197.2 %all-gather.13.cloned.1.call-start = ((), (), s32[]{:S(2)}) async-start(), calls=%async_computation.3 | async-start | bytes 7864320 | tf_op jit(solution)/shard_map/all_gather | solution.py:17
  15.3 344.6 %all-gather.9.cloned.1.call-start = ((), (), s32[]{:S(2)}) async-start(), calls=%async_computation.1 | async-start | bytes 16908288 | tf_op jit(solution)/shard_map/all_gather | solution.py:21
  212.4 189.0 %all-gather.11.cloned.1.call-start = ((), (), s32[]{:S(2)}) async-start(), calls=%async_computation.2 | async-start | bytes 7864320 | tf_op jit(solution)/shard_map/all_gather | solution.py:17
Sparse Core Ops, SparseCore 0:
  11.0 152.9 all-gather.6
  165.8 17.6 all-gather.12
  212.5 147.3 all-gather.8
  361.6 17.6 all-gather.10
where the time goes:
time: 416 us; the launch traced here: 415 us
  waiting for transfers between devices  295 us (71%)
  local copies, waits for them, and re-layouts  81.9 us (20%)
  between operations  13.2 us (3%)
  matrix products  12.2 us (3%)
  other arithmetic  11.8 us (3%)
    all_gather x2, waiting for transfers between devices, per_device(): gathered = lax.all_gather(current, 'cols', axis=1, tiled=True)  295 us
    reshape x2, local copies, waits for them, and re-layouts, per_device(): all_blocks = gathered.reshape(rows_here, nblocks_all, block_size)  45.3 us
    gather x2, local copies, waits for them, and re-layouts, per_device(): selected = jnp.take(all_blocks, pattern[layer].reshape(-1), axis=1)  26.9 us
    dot_general x2, matrix products, per_device(): jnp.einsum('sjkb,jkbc->sjc', picked, weight_used, preferred_element_type=...  12.2 us
    select_n x4, other arithmetic, per_device(): selected = jnp.take(all_blocks, pattern[layer].reshape(-1), axis=1)  10.7 us
  transfers between devices with their start and end apart: 4, of which 2 were waited for; matrix products, arithmetic and copies ran while one was open for 22% of the time, Pallas kernels for 0%

commit v1 on v0

v1 whole, which is shorter than its diff:
```python
import jax
import jax.numpy as jnp
from jax import lax
from jax.experimental import pallas as pl
from jax.experimental.pallas import tpu as pltpu
from jax.sharding import PartitionSpec as P

MESH = pl.DeviceIdType.MESH
NZ = 8
NQ = 4
OWN = 4
BLK = 128
HALF = 64
SLOTS = 40
LAYERS = 2
DEV = 128

A_TX, B_TX, BR_TX, C_TX, CR_TX = range(5)


def wrap(v, n):
    return lax.rem(v + n, n)


def kernel(
    act, w, bias, sel_v, sel_s, inv_s, out,
    gath, pack, recv, far, wts, acc, tab_v, tab_s,
    a_rx, b_rx, br_rx, c_rx, x_rx, tx, w_rx, w_tx, w_in, act_in, tab_rx, tab_tx, tab_in,
):
    me = lax.axis_index("cols")
    core = lax.axis_index("rows")
    sb = 8 + 24 * core
    sc = 32 - 24 * core
    z = lax.rem(me, NZ)
    b = lax.rem(lax.div(me, sb), NQ)
    c = lax.rem(lax.div(me, sc), NQ)

    def zdev(d):
        return me - z + wrap(z + d, NZ)

    def bdev(d):
        return me + (wrap(b + d, NQ) - b) * sb

    def cdev(d):
        return me + (wrap(c + d, NQ) - c) * sc

    def rcopy(src, dst, ssem, rsem, dev):
        return pltpu.make_async_remote_copy(
            src_ref=src, dst_ref=dst, send_sem=ssem, recv_sem=rsem,
            device_id={"cols": dev, "rows": core}, device_id_type=MESH,
        )

    def arrived(ref, sem):
        pltpu.make_async_copy(ref, ref, sem).wait()

    for h in range(2):
        for k in range(OWN):
            pltpu.make_async_copy(
                act.at[pl.ds(h * HALF, HALF), pl.ds(k * BLK, BLK)],
                gath.at[0, b, z, h, k], act_in,
            ).start()
    for l in range(LAYERS):
        pltpu.make_async_copy(
            w.at[l], wts.at[l, :, pl.ds(core * (SLOTS // 2), SLOTS // 2)], w_in.at[l]
        ).start()

    barrier = pltpu.get_barrier_semaphore()
    for dev in (zdev(1), zdev(-1), bdev(1), bdev(-1), cdev(1), cdev(-1), cdev(2)):
        pl.semaphore_signal(
            barrier, inc=1, device_id={"cols": dev, "rows": core}, device_id_type=MESH
        )
    pl.semaphore_signal(
        barrier, inc=1, device_id={"cols": me, "rows": 1 - core}, device_id_type=MESH
    )
    for l in range(LAYERS):
        for j in range(OWN):
            wts[l, j, SLOTS] = jnp.zeros((BLK, BLK), jnp.bfloat16)
    arrived(gath.at[0, b, z], act_in)
    pl.semaphore_wait(barrier, 8)

    table = [
        rcopy(sel_v, tab_v.at[0], tab_tx.at[0], tab_rx.at[0], cdev(-1)),
        rcopy(sel_v, tab_v.at[1], tab_tx.at[1], tab_rx.at[1], cdev(1)),
        rcopy(sel_v, tab_v.at[2], tab_tx.at[2], tab_rx.at[2], cdev(2)),
    ]
    for t in table:
        t.start()

    def wcopy(l):
        part = wts.at[l, :, pl.ds(core * (SLOTS // 2), SLOTS // 2)]
        return pltpu.make_async_remote_copy(
            src_ref=w.at[l], dst_ref=part, send_sem=w_tx.at[l], recv_sem=w_rx.at[l],
            device_id={"cols": me, "rows": 1 - core}, device_id_type=MESH,
        )

    def zidx(i):
        t = lax.div(i + 1, 2)
        return wrap(z + (1 - 2 * lax.rem(i, 2)) * t, NZ)

    def choose(blocks, which):
        picked = blocks[0]
        for k in range(1, OWN):
            picked = jnp.where(which == k, blocks[k], picked)
        return picked

    def send_picks(l, i, off):
        bb = wrap(b + off, NQ)
        zz = zidx(i)
        src = c * sc + bb * sb + zz
        right = tab_s[0, l, src]
        left = tab_s[1, l, src]
        over = tab_s[2, l, src]
        for h in range(2):
            blocks = [gath[l, bb, zz, h, k] for k in range(OWN)]
            pack[l, 0, i, off, h] = choose(blocks, right)
            pack[l, 1, i, off, h] = choose(blocks, left)
            pack[l, h, i, off, 2] = choose(blocks, over)
        for d in range(2):
            rcopy(
                pack.at[l, d, i, off], recv.at[l, d, i, off],
                tx.at[l, C_TX], c_rx.at[l, d, i, off], cdev(1 - 2 * d),
            ).start()

    def relay_picks(l, i, off):
        for d in range(2):
            arrived(recv.at[l, d, i, off], c_rx.at[l, d, i, off])
            rcopy(
                recv.at[l, d, i, off, 2], far.at[l, i, off, d],
                tx.at[l, CR_TX], x_rx.at[l, i], cdev(1 - 2 * d),
            ).start()

    def compute(l, i):
        zz = zidx(i)

        def step(off, carry):
            bb = wrap(b + off, NQ)
            base = bb * sb + zz
            own = sel_s[l * DEV + c * sc + base]
            x = jnp.concatenate(
                [
                    choose(
                        [gath[l, bb, zz, :, k].reshape(BLK, BLK) for k in range(OWN)], own
                    ),
                    recv[l, 0, i, off, pl.ds(0, 2)].reshape(BLK, BLK),
                    recv[l, 1, i, off, pl.ds(0, 2)].reshape(BLK, BLK),
                    far[l, i, off].reshape(BLK, BLK),
                ],
                axis=1,
            )
            rows = []
            for d in (0, -1, 1, 2):
                src = wrap(c + d, NQ) * sc + base
                rows.append(
                    jnp.concatenate(
                        [wts[l, j, inv_s[(l * OWN + j) * DEV + src]] for j in range(OWN)],
                        axis=1,
                    )
                )
            acc[...] += jnp.dot(
                x, jnp.concatenate(rows, axis=0), preferred_element_type=jnp.float32
            )
            return carry

        lax.fori_loop(0, NQ, step, 0)

    def layer(l, carry):
        acc[...] = jnp.zeros_like(acc)

        def turn(i, carry):
            @pl.when(i < NZ)
            def _():
                zz = zidx(i)
                unit = gath.at[l, b, zz]

                @pl.when(i == 0)
                def _():
                    for k, d in ((1, 1), (2, -1)):
                        rcopy(unit, unit, tx.at[l, A_TX], a_rx.at[l, k], zdev(d)).start()

                @pl.when(i >= 1)
                def _():
                    arrived(unit, a_rx.at[l, i])
                    way = 2 * lax.rem(i, 2) - 1

                    @pl.when(i < 5)
                    def _():
                        rcopy(
                            unit, unit, tx.at[l, A_TX], a_rx.at[l, i + 2], zdev(way)
                        ).start()

                    @pl.when((i == 5) | (i == 6))
                    def _():
                        part = gath.at[l, b, zz, i - 5]
                        rcopy(part, part, tx.at[l, A_TX], a_rx.at[l, 7], zdev(way)).start()

                for d in range(2):
                    rcopy(
                        unit, unit, tx.at[l, B_TX], b_rx.at[l, d, i], bdev(1 - 2 * d)
                    ).start()

                @pl.when((l == 0) & (i == 0))
                def _():
                    wcopy(0).start()
                    wcopy(1).start()
                    for t in table:
                        t.wait()
                    tab = pltpu.make_async_copy(tab_v, tab_s, tab_in)
                    tab.start()
                    tab.wait()

                send_picks(l, i, 0)

            @pl.when((i >= 1) & (i < NZ + 1))
            def _():
                j = i - 1
                zz = zidx(j)
                for d in range(2):
                    bb = wrap(b - 1 + 2 * d, NQ)
                    arrived(gath.at[l, bb, zz], b_rx.at[l, d, j])
                    part = gath.at[l, bb, zz, d]
                    rcopy(
                        part, part, tx.at[l, BR_TX], br_rx.at[l, j], bdev(1 - 2 * d)
                    ).start()
                send_picks(l, j, 1)
                send_picks(l, j, 3)

            @pl.when((i >= 2) & (i < NZ + 2))
            def _():
                j = i - 2
                arrived(gath.at[l, wrap(b + 2, NQ), zidx(j)], br_rx.at[l, j])
                send_picks(l, j, 2)

            @pl.when((i >= 1) & (i < NZ + 1))
            def _():
                relay_picks(l, i - 1, 0)

            @pl.when((i >= 2) & (i < NZ + 2))
            def _():
                relay_picks(l, i - 2, 1)
                relay_picks(l, i - 2, 3)

            @pl.when((i >= 3) & (i < NZ + 3))
            def _():
                relay_picks(l, i - 3, 2)

            @pl.when(i >= 4)
            def _():
                j = i - 4

                @pl.when((l == 0) & (j == 0))
                def _():
                    for k in range(LAYERS):
                        wcopy(k).wait_recv()
                        arrived(
                            wts.at[k, :, pl.ds(core * (SLOTS // 2), SLOTS // 2)],
                            w_in.at[k],
                        )

                arrived(far.at[l, j], x_rx.at[l, j])
                compute(l, j)

            return carry

        lax.fori_loop(0, NZ + 4, turn, 0)
        total = acc[...] + bias[pl.ds(l, 1), :]
        result = jnp.minimum(jnp.maximum(total, 0.0), 32.0).astype(jnp.bfloat16)

        @pl.when(l + 1 < LAYERS)
        def _():
            for h in range(2):
                for k in range(OWN):
                    gath[1, b, z, h, k] = result[
                        h * HALF : (h + 1) * HALF, k * BLK : (k + 1) * BLK
                    ]

        @pl.when(l + 1 == LAYERS)
        def _():
            out[...] = result

        return carry

    lax.fori_loop(0, LAYERS, layer, 0)
    for l in range(LAYERS):
        arrived(gath.at[l, 0, pl.ds(0, 7)], tx.at[l, A_TX])
        arrived(gath.at[l, pl.ds(0, 2)], tx.at[l, B_TX])
        arrived(gath.at[l, 0], tx.at[l, BR_TX])
        arrived(pack.at[l], tx.at[l, C_TX])
        arrived(far.at[l], tx.at[l, CR_TX])
        wcopy(l).wait_send()


def tables(pattern, counts):
    source = pattern // OWN
    chips = jnp.arange(DEV, dtype=jnp.int32)
    hit = source[..., None] == chips
    pick = jnp.max(jnp.where(hit, (pattern % OWN)[..., None], 0), axis=(1, 2))
    slot = jnp.arange(SLOTS, dtype=jnp.int32)[None, None, :, None]
    live = hit & (slot < counts[:, :, None, None])
    inverse = jnp.min(jnp.where(live, slot, SLOTS), axis=2)
    return pick, inverse


def per_device(activations, weights, biases, pattern, counts):
    pick, inverse = tables(pattern, counts)
    pick_v = jnp.pad(pick, ((0, 8 - LAYERS), (0, 0)))
    bf16, sem = jnp.bfloat16, pltpu.SemaphoreType.DMA
    vmem = pl.BlockSpec(memory_space=pltpu.VMEM)
    smem = pl.BlockSpec(memory_space=pltpu.SMEM)
    hbm = pl.BlockSpec(memory_space=pl.ANY)
    return pl.pallas_call(
        kernel,
        out_shape=jax.ShapeDtypeStruct(activations.shape, bf16),
        in_specs=[hbm, hbm, vmem, vmem, smem, smem],
        out_specs=vmem,
        scratch_shapes=[
            pltpu.VMEM((LAYERS, NQ, NZ, 2, OWN, HALF, BLK), bf16),
            pltpu.VMEM((LAYERS, 2, NZ, NQ, 3, HALF, BLK), bf16),
            pltpu.VMEM((LAYERS, 2, NZ, NQ, 3, HALF, BLK), bf16),
            pltpu.VMEM((LAYERS, NZ, NQ, 2, HALF, BLK), bf16),
            pltpu.VMEM((LAYERS, OWN, SLOTS + 1, BLK, BLK), bf16),
            pltpu.VMEM((2 * HALF, OWN * BLK), jnp.float32),
            pltpu.VMEM((3, 8, DEV), jnp.int32),
            pltpu.SMEM((3, 8, DEV), jnp.int32),
            sem((LAYERS, NZ)),
            sem((LAYERS, 2, NZ)),
            sem((LAYERS, NZ)),
            sem((LAYERS, 2, NZ, NQ)),
            sem((LAYERS, NZ)),
            sem((LAYERS, 5)),
            sem((LAYERS,)),
            sem((LAYERS,)),
            sem((LAYERS,)),
            sem,
            sem((3,)),
            sem((3,)),
            sem,
        ],
        compiler_params=pltpu.CompilerParams(
            collective_id=0, has_side_effects=True, vmem_limit_bytes=60 << 20
        ),
    )(activations, weights, biases, pick_v, pick.reshape(-1), inverse.reshape(-1))


def solution(mesh):
    return jax.shard_map(
        per_device,
        mesh=mesh,
        in_specs=(
            P("rows", "cols"),
            P(None, "cols", "rows", None, None),
            P(None, "cols"),
            P(None, "cols", None),
            P(None, "cols"),
        ),
        out_specs=P("rows", "cols"),
        check_vma=False,
    )
```

time: 416 us -> 116 us (0.28)
  waiting for transfers between devices: 295 us -> 0 us
  Pallas kernels: 0 us -> 111 us
  local copies, waits for them, and re-layouts: 81.9 us -> 2.16 us
  between operations: 13.2 us -> 0.01 us
  matrix products: 12.2 us -> 0 us
  other arithmetic: 11.8 us -> 2.25 us
    all_gather x4 -> x0, waiting for transfers between devices: 295 us -> none  [the longest x2 295 us: per_device(): gathered = lax.all_gather(current, 'cols', axis=1, tiled=True)]
    pallas_call x0 -> x1, Pallas kernels: none -> 111 us  [per_device(): pl.pallas_call(kernel, out_shape=jax.ShapeDtypeStruct(activations.shape,...]
    reshape x2 -> x0, local copies, waits for them, and re-layouts: 45.3 us -> none  [per_device(): all_blocks = gathered.reshape(rows_here, nblocks_all, block_size)]
    gather x2 -> x0, local copies, waits for them, and re-layouts: 26.9 us -> none  [per_device(): selected = jnp.take(all_blocks, pattern[layer].reshape(-1), axis=1)]
    dot_general x2 -> x0, matrix products: 12.2 us -> none  [per_device(): jnp.einsum('sjkb,jkbc->sjc', picked, weight_used, preferred_element_type=...]
    select_n x4 -> x1, other arithmetic: 10.7 us -> 0.7 us  [tables(): pick = jnp.max(jnp.where(hit, (pattern % OWN)[..., None], 0), axis=(1, 2))]
    slice x3 -> x0, local copies, waits for them, and re-layouts: 7.01 us -> none  [the longest x1 7 us: per_device(): weight_all = lax.all_gather(weights[layer], 'rows', axis=1, tiled=True)]
  transfers between devices with their start and end apart: 4 -> 0, of which waited for: 2 -> 0; matrix products, arithmetic and copies ran while one was open for 22% -> 0% of each run, Pallas kernels for 0% -> 0%
where the time goes in v1:
time: 116 us
  Pallas kernels  111 us (96%)
  other arithmetic  2.25 us (2%)
  local copies, waits for them, and re-layouts  2.16 us (2%)
    pallas_call x1, Pallas kernels, per_device(): pl.pallas_call(kernel, out_shape=jax.ShapeDtypeStruct(activations.shape,...  111 us

profile of v1, /device:TPU:8, one launch (start us, length us, event | category | flops | bytes accessed | tf_op | source)
XLA Modules:
  0.0 115.8 jit_solution(15341622723812222493)
XLA Ops:
  0.0 0.8 iota_compare_fusion.1
  0.8 0.7 add_select_fusion
  1.5 0.8 select_reduce_fusion
  2.3 0.0 copy-start
  2.3 0.6 pad.4.sel_v
  2.8 0.0 copy-done
  2.9 111.3 %shard_map.55 = bf16[128,512]{1,0:T(8,128)(2,1)} custom-call(bf16[128,512]{1,0:T(8,128)(2,1)} %act.1, bf16[2,4,20,128,128]{4,3,2,1,0:T(8,128)(2,1)} %w.1, f32[2,512]{1,0:T(2,128)} %bias.1, s32[8,128]{1,0:T(8,128)} %pad.4.sel_v, s32[256]{0:T(256)} %bitcast.3, s32[1024]{0:T(1024)} %bitcast.2), custom_call_target="tpu_custom_call" | custom-call | tf_op jit(solution)/shard_map/pallas_call | solution.py:310
  114.2 1.6 %copy.7 = bf16[128,512]{1,0:T(8,128)(2,1)} copy(bf16[128,512]{1,0:T(8,128)(2,1)} %shard_map.55) | data formatting | bytes 262144
Async XLA Ops:
  2.3 0.6 copy-start

commit v2 on v1

--- a/solution.py
+++ b/solution.py
@@ -15,7 +15,7 @@
 LAYERS = 2
 DEV = 128
 
-A_TX, B_TX, BR_TX, C_TX, CR_TX = range(5)
+A_TX, B_TX, BR_TX, C_TX, CR_TX, E_TX = range(6)
 
 
 def wrap(v, n):
@@ -25,7 +25,7 @@
 def kernel(
     act, w, bias, sel_v, sel_s, inv_s, out,
     gath, pack, recv, far, wts, acc, tab_v, tab_s,
-    a_rx, b_rx, br_rx, c_rx, x_rx, tx, w_rx, w_tx, w_in, act_in, tab_rx, tab_tx, tab_in,
+    a_rx, b_rx, br_rx, e_rx, c_rx, x_rx, tx, w_rx, w_tx, w_in, act_in, tab_rx, tab_tx, tab_in,
 ):
     me = lax.axis_index("cols")
     core = lax.axis_index("rows")
@@ -102,6 +102,33 @@
         for k in range(1, OWN):
             picked = jnp.where(which == k, blocks[k], picked)
         return picked
+
+    def relay_other(l, i, off):
+        bb = wrap(b + off, NQ)
+        unit = gath.at[l, bb, zidx(i), 1]
+
+        @pl.when(i == 0)
+        def _():
+            for k, d in ((1, 1), (2, -1)):
+                rcopy(unit, unit, tx.at[l, E_TX], e_rx.at[l, off - 1, k], zdev(d)).start()
+
+        @pl.when(i >= 1)
+        def _():
+            arrived(unit, e_rx.at[l, off - 1, i])
+            way = 2 * lax.rem(i, 2) - 1
+
+            @pl.when(i < 5)
+            def _():
+                rcopy(
+                    unit, unit, tx.at[l, E_TX], e_rx.at[l, off - 1, i + 2], zdev(way)
+                ).start()
+
+            @pl.when((i == 5) | (i == 6))
+            def _():
+                part = gath.at[l, bb, zidx(i), 1, pl.ds(2 * (i - 5), 2)]
+                rcopy(
+                    part, part, tx.at[l, E_TX], e_rx.at[l, off - 1, 7], zdev(way)
+                ).start()
 
     def send_picks(l, i, off):
         bb = wrap(b + off, NQ)
@@ -194,9 +221,18 @@
                         rcopy(part, part, tx.at[l, A_TX], a_rx.at[l, 7], zdev(way)).start()
 
                 for d in range(2):
-                    rcopy(
-                        unit, unit, tx.at[l, B_TX], b_rx.at[l, d, i], bdev(1 - 2 * d)
-                    ).start()
+                    @pl.when(i == 0)
+                    def _():
+                        rcopy(
+                            unit, unit, tx.at[l, B_TX], b_rx.at[l, d, i], bdev(1 - 2 * d)
+                        ).start()
+
+                    @pl.when(i >= 1)
+                    def _():
+                        part = gath.at[l, b, zz, 0]
+                        rcopy(
+                            part, part, tx.at[l, B_TX], b_rx.at[l, d, i], bdev(1 - 2 * d)
+                        ).start()
 
                 @pl.when((l == 0) & (i == 0))
                 def _():
@@ -216,18 +252,40 @@
                 zz = zidx(j)
                 for d in range(2):
                     bb = wrap(b - 1 + 2 * d, NQ)
-                    arrived(gath.at[l, bb, zz], b_rx.at[l, d, j])
-                    part = gath.at[l, bb, zz, d]
-                    rcopy(
-                        part, part, tx.at[l, BR_TX], br_rx.at[l, j], bdev(1 - 2 * d)
-                    ).start()
+
+                    @pl.when(j == 0)
+                    def _():
+                        arrived(gath.at[l, bb, zz], b_rx.at[l, d, j])
+                        part = gath.at[l, bb, zz, d]
+                        rcopy(
+                            part, part, tx.at[l, BR_TX], br_rx.at[l, j], bdev(1 - 2 * d)
+                        ).start()
+
+                    @pl.when(j >= 1)
+                    def _():
+                        arrived(gath.at[l, bb, zz, 0], b_rx.at[l, d, j])
+                        part = gath.at[l, bb, zz, 0, pl.ds(2 * d, 2)]
+                        rcopy(
+                            part, part, tx.at[l, BR_TX], br_rx.at[l, j], bdev(1 - 2 * d)
+                        ).start()
+                relay_other(l, j, 1)
+                relay_other(l, j, 3)
                 send_picks(l, j, 1)
                 send_picks(l, j, 3)
 
             @pl.when((i >= 2) & (i < NZ + 2))
             def _():
                 j = i - 2
-                arrived(gath.at[l, wrap(b + 2, NQ), zidx(j)], br_rx.at[l, j])
+
+                @pl.when(j == 0)
+                def _():
+                    arrived(gath.at[l, wrap(b + 2, NQ), zidx(j)], br_rx.at[l, j])
+
+                @pl.when(j >= 1)
+                def _():
+                    arrived(gath.at[l, wrap(b + 2, NQ), zidx(j), 0], br_rx.at[l, j])
+
+                relay_other(l, j, 2)
                 send_picks(l, j, 2)
 
             @pl.when((i >= 1) & (i < NZ + 1))
@@ -282,8 +340,9 @@
     lax.fori_loop(0, LAYERS, layer, 0)
     for l in range(LAYERS):
         arrived(gath.at[l, 0, pl.ds(0, 7)], tx.at[l, A_TX])
-        arrived(gath.at[l, pl.ds(0, 2)], tx.at[l, B_TX])
-        arrived(gath.at[l, 0], tx.at[l, BR_TX])
+        arrived(gath.at[l, pl.ds(0, 3), pl.ds(0, 3)], tx.at[l, B_TX])
+        arrived(gath.at[l, pl.ds(0, 3), pl.ds(0, 3), 0], tx.at[l, BR_TX])
+        arrived(gath.at[l, pl.ds(0, 3), pl.ds(0, 7), 0], tx.at[l, E_TX])
         arrived(pack.at[l], tx.at[l, C_TX])
         arrived(far.at[l], tx.at[l, CR_TX])
         wcopy(l).wait_send()
@@ -324,9 +383,10 @@
             sem((LAYERS, NZ)),
             sem((LAYERS, 2, NZ)),
             sem((LAYERS, NZ)),
+            sem((LAYERS, NQ - 1, NZ)),
             sem((LAYERS, 2, NZ, NQ)),
             sem((LAYERS, NZ)),
-            sem((LAYERS, 5)),
+            sem((LAYERS, 6)),
             sem((LAYERS,)),
             sem((LAYERS,)),
             sem((LAYERS,)),

time: 116 us -> 111 us (0.957)
  Pallas kernels: 111 us -> 106 us
    pallas_call x1, Pallas kernels: 111 us -> 106 us  [per_device(): pl.pallas_call(kernel, out_shape=jax.ShapeDtypeStruct(activations.shape,...]
where the time goes in v2:
time: 111 us
  Pallas kernels  106 us (95%)
  other arithmetic  2.25 us (2%)
  local copies, waits for them, and re-layouts  2.16 us (2%)
    pallas_call x1, Pallas kernels, per_device(): pl.pallas_call(kernel, out_shape=jax.ShapeDtypeStruct(activations.shape,...  106 us

profile of v2, /device:TPU:8, one launch (start us, length us, event | category | flops | bytes accessed | tf_op | source)
XLA Modules:
  0.0 110.5 jit_solution(8234414873650936185)
XLA Ops:
  0.0 0.8 iota_compare_fusion.1
  0.8 0.7 add_select_fusion
  1.5 0.8 select_reduce_fusion
  2.3 0.0 copy-start
  2.3 0.6 pad.4.sel_v
  2.8 0.0 copy-done
  2.9 106.1 %shard_map.55 = bf16[128,512]{1,0:T(8,128)(2,1)} custom-call(bf16[128,512]{1,0:T(8,128)(2,1)} %act.1, bf16[2,4,20,128,128]{4,3,2,1,0:T(8,128)(2,1)} %w.1, f32[2,512]{1,0:T(2,128)} %bias.1, s32[8,128]{1,0:T(8,128)} %pad.4.sel_v, s32[256]{0:T(256)} %bitcast.3, s32[1024]{0:T(1024)} %bitcast.2), custom_call_target="tpu_custom_call" | custom-call | tf_op jit(solution)/shard_map/pallas_call | solution.py:369
  108.9 1.6 %copy.7 = bf16[128,512]{1,0:T(8,128)(2,1)} copy(bf16[128,512]{1,0:T(8,128)(2,1)} %shard_map.55) | data formatting | bytes 262144
Async XLA Ops:
  2.3 0.6 copy-start

commit v3 on v2

--- a/solution.py
+++ b/solution.py
@@ -349,10 +349,10 @@
 
 
 def tables(pattern, counts):
-    source = pattern // OWN
+    source = pattern >> 2
     chips = jnp.arange(DEV, dtype=jnp.int32)
     hit = source[..., None] == chips
-    pick = jnp.max(jnp.where(hit, (pattern % OWN)[..., None], 0), axis=(1, 2))
+    pick = jnp.max(jnp.where(hit, (pattern & (OWN - 1))[..., None], 0), axis=(1, 2))
     slot = jnp.arange(SLOTS, dtype=jnp.int32)[None, None, :, None]
     live = hit & (slot < counts[:, :, None, None])
     inverse = jnp.min(jnp.where(live, slot, SLOTS), axis=2)
@@ -361,7 +361,6 @@
 
 def per_device(activations, weights, biases, pattern, counts):
     pick, inverse = tables(pattern, counts)
-    pick_v = jnp.pad(pick, ((0, 8 - LAYERS), (0, 0)))
     bf16, sem = jnp.bfloat16, pltpu.SemaphoreType.DMA
     vmem = pl.BlockSpec(memory_space=pltpu.VMEM)
     smem = pl.BlockSpec(memory_space=pltpu.SMEM)
@@ -378,8 +377,8 @@
             pltpu.VMEM((LAYERS, NZ, NQ, 2, HALF, BLK), bf16),
             pltpu.VMEM((LAYERS, OWN, SLOTS + 1, BLK, BLK), bf16),
             pltpu.VMEM((2 * HALF, OWN * BLK), jnp.float32),
-            pltpu.VMEM((3, 8, DEV), jnp.int32),
-            pltpu.SMEM((3, 8, DEV), jnp.int32),
+            pltpu.VMEM((3, LAYERS, DEV), jnp.int32),
+            pltpu.SMEM((3, LAYERS, DEV), jnp.int32),
             sem((LAYERS, NZ)),
             sem((LAYERS, 2, NZ)),
             sem((LAYERS, NZ)),
@@ -398,7 +397,7 @@
         compiler_params=pltpu.CompilerParams(
             collective_id=0, has_side_effects=True, vmem_limit_bytes=60 << 20
         ),
-    )(activations, weights, biases, pick_v, pick.reshape(-1), inverse.reshape(-1))
+    )(activations, weights, biases, pick, pick.reshape(-1), inverse.reshape(-1))
 
 
 def solution(mesh):

time: 111 us -> 111 us (level)
  no operation moved by 1% of the time
where the time goes in v3:
time: 111 us; the launch traced here: 110 us
  Pallas kernels  106 us (95%)
  other arithmetic  2.25 us (2%)
  local copies, waits for them, and re-layouts  1.57 us (1%)
    pallas_call x1, Pallas kernels, per_device(): pl.pallas_call(kernel, out_shape=jax.ShapeDtypeStruct(activations.shape,...  106 us

profile of v3, /device:TPU:8, one launch (start us, length us, event | category | flops | bytes accessed | tf_op | source)
XLA Modules:
  0.0 109.9 jit_solution(16887229189177754188)
XLA Ops:
  0.0 0.8 iota_compare_fusion.1
  0.8 0.7 broadcast_and_fusion
  1.4 0.8 select_reduce_fusion
  2.2 106.0 %shard_map.55 = bf16[128,512]{1,0:T(8,128)(2,1)} custom-call(bf16[128,512]{1,0:T(8,128)(2,1)} %act.1, bf16[2,4,20,128,128]{4,3,2,1,0:T(8,128)(2,1)} %w.1, f32[2,512]{1,0:T(2,128)} %bias.1, s32[2,128]{1,0:T(2,128)} %get-tuple-element.6.sel_v, s32[256]{0:T(256)} %bitcast.3, s32[1024]{0:T(1024)} %bitcast.2), custom_call_target="tpu_custom_call" | custom-call | tf_op jit(solution)/shard_map/pallas_call | solution.py:368
  108.3 1.6 %copy.7 = bf16[128,512]{1,0:T(8,128)(2,1)} copy(bf16[128,512]{1,0:T(8,128)(2,1)} %shard_map.55) | data formatting | bytes 262144
